TPU v7x, 32 devices: a whole 2x2x4 slice. The times are simulated.
32 devices in a mesh: rep: 8 (over y, x, core), fsdp: 4 (over z).
Axes of the slice: x: 2, y: 2, z: 4, core: 2. Of those that a mesh axis runs over, the one named last changes fastest.
Arguments:
- images: bfloat16 [8, 16, 128, 768], P('rep', 'fsdp'), may hold values from -6 to 6
- cotangent: bfloat16 [8, 16, 128, 1536], P('rep', 'fsdp'), may hold values from -6 to 6
- params: float32 [8, 768, 1536], P('rep', 'fsdp'), may hold values from -6 to 6
- counts: int32 [8, 4], P('rep'), may hold values from 1 to 4, 9 in all within a row
- partner: int32 [8], P('rep'), may hold values from 0 to 7, as said below
- ln_gain: float32 [768], replicated, may hold values from 0.1 to 1.9
- ln_bias: float32 [768], replicated, may hold values from -3 to 3
- expand_bias: float32 [1536], replicated, may hold values from -4 to 4
Outputs:
- new_params: float32 [8, 768, 1536], P('rep', 'fsdp')
Inputs may be any that keep to these rules, and one draw needn't show every extreme that they name: The 4 counts of a replica sum to 9; some group holds 4 live images. partner[partner[r]] equals r, and partner[r] is r or (r + 4) modulo 8.
All inputs are finite; a program needn't handle non-finite values.
Results may differ from a plain program's by a relative error of at most 0.0045.
Values may be sent and summed in bfloat16 or wider, within the bound.
A program may use at most 64 MiB of HBM per device.

v0:
```python
import functools

import jax
import jax.numpy as jnp
from jax import lax
from jax.experimental import pallas as pl
from jax.experimental.pallas import tpu as pltpu
from jax.sharding import PartitionSpec as P

eps_norm = 1e-06
learn_rate = 0.5
CHUNK = 128
DEPTH = 1.0
PRI = dict(
    own=-13.95, fwd=-13.04, fwd_far=-4.93, comp=-1.0, sum=-2.09, sum_far=-6.79, sum_hop=13.66,
    fin=-5.34, merge=-2.93, norm=10.81,
)
MESH_ID = pl.DeviceIdType.MESH


def plan(n, widths, pri, depth, rate=120.0, lat=2.2, cost=0.06):
    last = n - 1
    pieces = len(widths)
    dur = [w / rate + cost for w in widths]
    arrive = [dict() for _ in range(n)]
    now = [2.0] * n
    link = [dict(u=0.0, d=0.0, y=0.0) for _ in range(n)]
    todo, orders = [], [[] for _ in range(n)]
    for z in range(n):
        mine = []
        for k in range(pieces):
            if z < last: mine.append(("own", k, z, "u"))
            if z > 0: mine.append(("own", k, z, "d"))
            for s in range(n):
                if s != z: mine.append(("fwd", k, s, "u" if s < z else "d"))
            mine.append(("comp", k, 0, ""))
            for j in range(z + 1, n): mine.append(("sum", k, j, "u"))
            for j in range(z): mine.append(("sum", k, j, "d"))
            mine.append(("fin", k, z, "y"))
            mine.append(("merge", k, z, ""))
        mine.append(("norm", 0, 0, ""))
        todo.append(mine)
    done = [set() for _ in range(n)]
    def rank(z, t):
        kind, k, j, way = t
        far = abs(j - z)
        if kind == "own": return k + pri["own"]
        if kind == "fwd": return k + pri["fwd"] + (far - 1) * pri["fwd_far"]
        if kind == "sum": return k + pri["sum"] + far * pri["sum_far"] + (z if way == "u" else last - z) * pri["sum_hop"]
        return k + pri.get(kind, 0.0)
    def ready(z, t):
        kind, k, j, way = t
        a, d = arrive[z], done[z]
        times = [0.0]
        inf = float("inf")
        if kind == "fwd":
            times.append(a.get(("a", k, j), inf))
        elif kind == "comp":
            if ("norm", 0, 0, "") not in d: return inf
            if k and ("comp", k - 1, 0, "") not in d: return inf
            for s in range(n):
                if s != z and ("fwd", k, s, "u" if s < z else "d") not in d: return inf
        elif kind in ("sum", "fin"):
            if ("comp", k, 0, "") not in d: return inf
            if kind == "sum" and (z > 0 if way == "u" else z < last): times.append(a.get((way, k, j), inf))
            if kind == "fin":
                if z > 0: times.append(a.get(("u", k, z), inf))
                if z < last: times.append(a.get(("d", k, z), inf))
        elif kind == "merge":
            if ("fin", k, z, "y") not in d: return inf
            times.append(a.get(("y", k, z), inf))
        sends = kind in ("own", "sum") or (kind == "fwd" and (z < last if way == "u" else z > 0))
        if sends: times.append(link[z][way] - depth * dur[k])
        return max(times)
    while any(todo):
        best = None
        for z in range(n):
            if not todo[z]: continue
            r = [(ready(z, t), t) for t in todo[z]]
            t0 = max(now[z], min(r)[0])
            if t0 == float("inf"): continue
            if best is None or t0 < best[0]:
                best = (t0, z, min((t for e, t in r if e <= t0), key=lambda t: (rank(z, t), t)))
        t0, z, t = best
        kind, k, j, way = t
        todo[z].remove(t); done[z].add(t); orders[z].append(t)
        spend = {"own": .03, "fwd": .05, "comp": widths[k] / 110.0, "sum": .12, "fin": .15, "merge": .15, "norm": 2.0}[kind]
        now[z] = t0 + spend
        to = None
        if kind == "own" or kind == "fwd": to, tag = z + (1 if way == "u" else -1), ("a", k, j)
        elif kind == "sum": to, tag = z + (1 if way == "u" else -1), (way, k, j)
        elif kind == "fin": to, tag = z, ("y", k, z)
        if to is not None and 0 <= to <= last:
            start = max(link[z][way], now[z])
            link[z][way] = start + dur[k]
            arrive[to][tag] = start + dur[k] + lat
    return max(now), orders


def gelu_slope(x):
    cdf = 0.5 * (1.0 + lax.erf(x * 0.7071067811865476))
    return cdf + x * (jnp.exp(-0.5 * x * x) * 0.3989422804014327)


def body(
    n, reps, pieces,
    count_ref, partner_ref, images, cotangent, weights, gain_in, bias_in, ebias_in,
    out_ref,
    gain_ref, bias_ref, ebias_ref, img, cot, par, x, xt, wfull, delta, part, u_in, d_in, u_out, d_out, acc,
    far_out, far_in, merged,
    in_sem, ag_recv, ag_up, ag_dn, u_send, u_recv, d_send, d_recv, y_send, y_recv, o_sem,
):
    z = lax.axis_index("fsdp")
    rep = lax.axis_index("rep")
    partner = {"rep": lax.rem(rep + reps // 2, reps)}
    up, down = {"fsdp": z + 1}, {"fsdp": z - 1}
    last = n - 1
    slots, per_image, width = images.shape
    depth = width // n
    cols = wfull.shape[-1]
    scale = float(width) ** (-0.5)

    load_w = pltpu.make_async_copy(weights, par, in_sem.at[0])
    load_x = pltpu.make_async_copy(images, img, in_sem.at[1])
    load_c = pltpu.make_async_copy(cotangent, cot, in_sem.at[2])
    small = [
        pltpu.make_async_copy(gain_in, gain_ref, in_sem.at[3]),
        pltpu.make_async_copy(bias_in, bias_ref, in_sem.at[4]),
        pltpu.make_async_copy(ebias_in, ebias_ref, in_sem.at[5]),
    ]
    load_w.start()
    load_x.start()
    for load in small:
        load.start()
    load_c.start()

    barrier = pltpu.get_barrier_semaphore()

    @pl.when(z < last)
    def _():
        pl.semaphore_signal(barrier, inc=1, device_id=up, device_id_type=MESH_ID)

    @pl.when(z > 0)
    def _():
        pl.semaphore_signal(barrier, inc=1, device_id=down, device_id_type=MESH_ID)

    pl.semaphore_signal(barrier, inc=1, device_id=partner, device_id_type=MESH_ID)

    load_w.wait()
    for k in range(pieces):
        wfull[k, z] = par[:, k * cols:(k + 1) * cols].astype(jnp.bfloat16)

    peers = 1 + (z > 0).astype(jnp.int32) + (z < last).astype(jnp.int32)
    pl.semaphore_wait(barrier, peers)

    def remote(src, dst, send, recv, to):
        return pltpu.make_async_remote_copy(
            src_ref=src, dst_ref=dst, send_sem=send, recv_sem=recv,
            device_id=to, device_id_type=MESH_ID,
        )

    def ag_copy(k, s, to, send):
        return remote(wfull.at[k, s], wfull.at[k, s], send.at[k, s], ag_recv.at[k, s], to)

    def u_copy(k, j):
        return remote(u_out.at[k, j], u_in.at[k, j], u_send.at[k, j], u_recv.at[k, j], up)

    def d_copy(k, j):
        return remote(d_out.at[k, j], d_in.at[k, j], d_send.at[k, j], d_recv.at[k, j], down)

    def y_copy(k):
        return remote(far_out.at[k], far_in.at[k], y_send.at[k], y_recv.at[k], partner)

    def out_copy(k):
        span = pl.ds(k * cols, cols)
        return pltpu.make_async_copy(merged.at[k], out_ref.at[:, span], o_sem.at[k])

    def norm():
        load_x.wait()
        for load in small:
            load.wait()
        gain = gain_ref[...][None, :]
        shift = bias_ref[...][None, :]
        for i in range(slots):
            rows = img[i].astype(jnp.float32)
            mean = jnp.mean(rows, axis=-1, keepdims=True)
            centered = rows - mean
            var = jnp.mean(centered * centered, axis=-1, keepdims=True)
            v = centered * lax.rsqrt(var + eps_norm) * gain + shift
            x[i] = v.astype(jnp.bfloat16)
            xt[:, i * per_image:(i + 1) * per_image] = v.T.astype(jnp.bfloat16)
        load_c.wait()

    count = count_ref[0, z]
    mix = jnp.where(partner_ref[0] != rep, 0.5, 0.0).astype(jnp.float32)

    def compute(k):
        lo = k * cols
        w = wfull.at[k]
        extra = ebias_ref[lo:lo + cols][None, :]

        def one(i, carry):
            pre = jnp.dot(
                x[i], w[...].reshape(width, cols), preferred_element_type=jnp.float32
            )
            pre = pre * scale + extra
            live = jnp.where(i < count, 1.0, 0.0).astype(jnp.float32)
            cur = cot[i, :, lo:lo + cols].astype(jnp.float32)
            rows = pl.ds(pl.multiple_of(i * per_image, per_image), per_image)
            delta[rows, :] = (cur * gelu_slope(pre) * live).astype(jnp.bfloat16)
            return carry

        lax.fori_loop(0, slots, one, 0)

        def two(j, carry):
            rows = pl.ds(pl.multiple_of(j * depth, depth), depth)
            part[k, j] = scale * jnp.dot(
                xt[rows, :], delta[...], preferred_element_type=jnp.float32
            )
            return carry

        lax.fori_loop(0, n, two, 0)

    def step(me, kind, k, j, way):
        to, send = (up, ag_up) if way == "u" else (down, ag_dn)
        copy, came, out = (u_copy, u_in, u_out) if way == "u" else (d_copy, d_in, d_out)
        final = me == (last if way == "u" else 0)
        first = me == (0 if way == "u" else last)
        if kind == "own":
            ag_copy(k, me, to, send).start()
        elif kind == "fwd":
            ag_copy(k, j, to, send).wait_recv()
            if not final:
                ag_copy(k, j, to, send).start()
        elif kind == "sum":
            total = part[k, j]
            if not first:
                copy(k, j).wait_recv()
                total = total + came[k, j].astype(jnp.float32)
            out[k, j] = total.astype(jnp.bfloat16)
            copy(k, j).start()
        elif kind == "fin":
            total = part[k, me]
            if me > 0:
                u_copy(k, me).wait_recv()
                total = total + u_in[k, me].astype(jnp.float32)
            if me < last:
                d_copy(k, me).wait_recv()
                total = total + d_in[k, me].astype(jnp.float32)
            stepped = par[:, k * cols:(k + 1) * cols] - learn_rate * total
            acc[k] = stepped
            far_out[k] = stepped.astype(jnp.bfloat16)
            y_copy(k).start()
        elif kind == "merge":
            y_copy(k).wait_recv()
            stepped = acc[k]
            merged[k] = stepped + mix * (far_in[k].astype(jnp.float32) - stepped)
            out_copy(k).start()

    _, orders = plan(n, [cols] * pieces, PRI, DEPTH)
    segments = []
    for order in orders:
        parts = [[]]
        for entry in order:
            if entry[0] in ("norm", "comp"):
                parts.append([])
            else:
                parts[-1].append(entry)
        segments.append(parts)
    for stage in range(pieces + 2):
        for me in range(n):
            @pl.when(z == me)
            def _():
                for entry in segments[me][stage]:
                    step(me, *entry)
        if stage == 0:
            norm()
        elif stage <= pieces:
            compute(stage - 1)

    for k in range(pieces):
        for s in range(n):
            @pl.when((z < last) & (s <= z))
            def _():
                ag_copy(k, s, up, ag_up).wait_send()

            @pl.when((z > 0) & (s >= z))
            def _():
                ag_copy(k, s, down, ag_dn).wait_send()

            @pl.when(s > z)
            def _():
                u_copy(k, s).wait_send()

            @pl.when(s < z)
            def _():
                d_copy(k, s).wait_send()

        y_copy(k).wait_send()
        out_copy(k).wait()


def shards(n, reps, images, cotangent, params, counts, partner, ln_gain, ln_bias, expand_bias):
    _, slots, per_image, width = images.shape
    hidden = cotangent.shape[-1]
    depth = params.shape[1]
    cols = CHUNK
    pieces = hidden // cols
    rows = slots * per_image
    scalars = pl.BlockSpec(memory_space=pltpu.SMEM)
    anywhere = pl.BlockSpec(memory_space=pl.ANY)
    dma = pltpu.SemaphoreType.DMA
    bf, f32 = jnp.bfloat16, jnp.float32
    piece = (pieces, n, depth, cols)
    merged = pl.pallas_call(
        functools.partial(body, n, reps, pieces),
        out_shape=jax.ShapeDtypeStruct((depth, hidden), f32),
        in_specs=[scalars] * 2 + [anywhere] * 6,
        out_specs=anywhere,
        scratch_shapes=[
            pltpu.VMEM((width,), f32),
            pltpu.VMEM((width,), f32),
            pltpu.VMEM((hidden,), f32),
            pltpu.VMEM((slots, per_image, width), bf),
            pltpu.VMEM((slots, per_image, hidden), bf),
            pltpu.VMEM((depth, hidden), f32),
            pltpu.VMEM((slots, per_image, width), bf),
            pltpu.VMEM((width, rows), bf),
            pltpu.VMEM(piece, bf),
            pltpu.VMEM((rows, cols), bf),
            pltpu.VMEM(piece, f32),
            pltpu.VMEM(piece, bf),
            pltpu.VMEM(piece, bf),
            pltpu.VMEM(piece, bf),
            pltpu.VMEM(piece, bf),
            pltpu.VMEM((pieces, depth, cols), f32),
            pltpu.VMEM((pieces, depth, cols), bf),
            pltpu.VMEM((pieces, depth, cols), bf),
            pltpu.VMEM((pieces, depth, cols), f32),
            dma((6,)),
        ] + [dma((pieces, n))] * 7 + [dma((pieces,))] * 3,
        compiler_params=pltpu.CompilerParams(
            collective_id=0, has_side_effects=True, vmem_limit_bytes=62 * 1024 * 1024
        ),
    )(
        counts, partner, images[0], cotangent[0], params[0], ln_gain, ln_bias, expand_bias,
    )
    return merged[None]


def solution(mesh):
    in_specs = (
        P("rep", "fsdp", None, None),
        P("rep", "fsdp", None, None),
        P("rep", "fsdp", None),
        P("rep", None),
        P("rep"),
        P(),
        P(),
        P(),
    )
    out_specs = P("rep", "fsdp", None)
    return jax.shard_map(
        functools.partial(shards, mesh.shape["fsdp"], mesh.shape["rep"]),
        mesh=mesh, in_specs=in_specs, out_specs=out_specs, check_vma=False,
    )
```

profile of v0, /device:TPU:0, one launch (start us, length us, event | category | flops | bytes accessed | tf_op | source)
XLA Modules:
  0.0 70.2 jit_solution(5229722824266810186)
XLA Ops:
  0.7 67.2 %shard_map.82 = f32[192,1536]{1,0:T(8,128)} custom-call(s32[1,4]{1,0:T(1,128)} %count_ref.1, s32[1]{0:T(128)S(6)} %copy.10.partner_ref, bf16[4,128,768]{2,1,0:T(8,128)(2,1)} %bitcast.7, bf16[4,128,1536]{2,1,0:T(8,128)(2,1)} %bitcast.5, f32[192,1536]{1,0:T(8,128)} %bitcast.6, f32[768]{0:T(1024)} %gain_in.1, f32[768]{0:T(1024)} %bias_in.1, f32[1536]{0:T(1024)} %ebias_in.1), custom_call_target="tpu_custom_call" | custom-call | tf_op jit(solution)/shard_map/pallas_call | solution.py:315
  67.8 2.4 %copy.11 = f32[1,192,1536]{2,1,0:T(8,128)} copy(f32[1,192,1536]{2,1,0:T(8,128)} %bitcast.4) | data formatting | bytes 2359296
where the time goes:
time: 70.3 us; the launch traced here: 70.2 us
  Pallas kernels  67.2 us (96%)
  local copies, waits for them, and re-layouts  2.36 us (3%)
    pallas_call x1, Pallas kernels, shards(): pl.pallas_call(functools.partial(body, n, reps, pieces), out_shape=jax.Sh...  67.2 us
    unnamed x1, local copies, waits for them, and re-layouts  2.36 us

commit v1 on v0

--- a/solution.py
+++ b/solution.py
@@ -104,11 +104,11 @@
 
 def body(
     n, reps, pieces,
-    count_ref, partner_ref, images, cotangent, weights, gain_in, bias_in, ebias_in,
+    partner_ref, count_in, images, cotangent, weights, gain_in, bias_in, ebias_in,
     out_ref,
     gain_ref, bias_ref, ebias_ref, img, cot, par, x, xt, wfull, delta, part, u_in, d_in, u_out, d_out, acc,
-    far_out, far_in, merged,
-    in_sem, ag_recv, ag_up, ag_dn, u_send, u_recv, d_send, d_recv, y_send, y_recv, o_sem,
+    far_out, far_in,
+    count_ref, in_sem, z_recv, y_recv, sent,
 ):
     z = lax.axis_index("fsdp")
     rep = lax.axis_index("rep")
@@ -120,35 +120,58 @@
     cols = wfull.shape[-1]
     scale = float(width) ** (-0.5)
 
-    load_w = pltpu.make_async_copy(weights, par, in_sem.at[0])
+    _, orders = plan(n, [cols] * pieces, PRI, DEPTH)
+    segments = []
+    for order in orders:
+        parts = [[]]
+        for entry in order:
+            if entry[0] in ("norm", "comp"):
+                parts.append([])
+            else:
+                parts[-1].append(entry)
+        segments.append(parts)
+    early = 1 + max(entry[1] for parts in segments for entry in parts[0])
+
+    def load_cols(lo, hi, sem):
+        span = pl.ds(lo * cols, (hi - lo) * cols)
+        return pltpu.make_async_copy(weights.at[:, span], par.at[:, span], sem)
+
+    load_w = load_cols(0, early, in_sem.at[0])
+    load_rest = load_cols(early, pieces, in_sem.at[6])
     load_x = pltpu.make_async_copy(images, img, in_sem.at[1])
     load_c = pltpu.make_async_copy(cotangent, cot, in_sem.at[2])
     small = [
         pltpu.make_async_copy(gain_in, gain_ref, in_sem.at[3]),
         pltpu.make_async_copy(bias_in, bias_ref, in_sem.at[4]),
         pltpu.make_async_copy(ebias_in, ebias_ref, in_sem.at[5]),
+        pltpu.make_async_copy(count_in, count_ref, in_sem.at[7]),
     ]
     load_w.start()
+
+    barrier = pltpu.get_barrier_semaphore()
+
+    @pl.when(z < last)
+    def _():
+        pl.semaphore_signal(barrier, inc=1, device_id=up, device_id_type=MESH_ID)
+
+    @pl.when(z > 0)
+    def _():
+        pl.semaphore_signal(barrier, inc=1, device_id=down, device_id_type=MESH_ID)
+
+    pl.semaphore_signal(barrier, inc=1, device_id=partner, device_id_type=MESH_ID)
+
+    load_rest.start()
     load_x.start()
     for load in small:
         load.start()
     load_c.start()
 
-    barrier = pltpu.get_barrier_semaphore()
-
-    @pl.when(z < last)
-    def _():
-        pl.semaphore_signal(barrier, inc=1, device_id=up, device_id_type=MESH_ID)
-
-    @pl.when(z > 0)
-    def _():
-        pl.semaphore_signal(barrier, inc=1, device_id=down, device_id_type=MESH_ID)
-
-    pl.semaphore_signal(barrier, inc=1, device_id=partner, device_id_type=MESH_ID)
+    def cast(k):
+        wfull[k, z] = par[:, k * cols:(k + 1) * cols].astype(jnp.bfloat16)
 
     load_w.wait()
-    for k in range(pieces):
-        wfull[k, z] = par[:, k * cols:(k + 1) * cols].astype(jnp.bfloat16)
+    for k in range(early):
+        cast(k)
 
     peers = 1 + (z > 0).astype(jnp.int32) + (z < last).astype(jnp.int32)
     pl.semaphore_wait(barrier, peers)
@@ -159,23 +182,25 @@
             device_id=to, device_id_type=MESH_ID,
         )
 
+    ag_up, ag_dn, u_send, d_send, y_send = (sent.at[i] for i in range(5))
+
     def ag_copy(k, s, to, send):
-        return remote(wfull.at[k, s], wfull.at[k, s], send.at[k, s], ag_recv.at[k, s], to)
-
-    def u_copy(k, j):
-        return remote(u_out.at[k, j], u_in.at[k, j], u_send.at[k, j], u_recv.at[k, j], up)
-
-    def d_copy(k, j):
-        return remote(d_out.at[k, j], d_in.at[k, j], d_send.at[k, j], d_recv.at[k, j], down)
+        return remote(wfull.at[k, s], wfull.at[k, s], send, z_recv.at[k, s], to)
+
+    def u_copy(k, j, here):
+        return remote(u_out.at[k, j], u_in.at[k, j], u_send, z_recv.at[k, j], up)
+
+    def d_copy(k, j, here):
+        sem = z_recv.at[k, n if j == here else j]
+        return remote(d_out.at[k, j], d_in.at[k, j], d_send, sem, down)
 
     def y_copy(k):
-        return remote(far_out.at[k], far_in.at[k], y_send.at[k], y_recv.at[k], partner)
-
-    def out_copy(k):
-        span = pl.ds(k * cols, cols)
-        return pltpu.make_async_copy(merged.at[k], out_ref.at[:, span], o_sem.at[k])
+        return remote(far_out.at[k], far_in.at[k], y_send, y_recv.at[k], partner)
 
     def norm():
+        load_rest.wait()
+        for k in range(early, pieces):
+            cast(k)
         load_x.wait()
         for load in small:
             load.wait()
@@ -191,8 +216,8 @@
             xt[:, i * per_image:(i + 1) * per_image] = v.T.astype(jnp.bfloat16)
         load_c.wait()
 
-    count = count_ref[0, z]
-    mix = jnp.where(partner_ref[0] != rep, 0.5, 0.0).astype(jnp.float32)
+    def mix():
+        return jnp.where(partner_ref[0] != rep, 0.5, 0.0).astype(jnp.float32)
 
     def compute(k):
         lo = k * cols
@@ -204,7 +229,7 @@
                 x[i], w[...].reshape(width, cols), preferred_element_type=jnp.float32
             )
             pre = pre * scale + extra
-            live = jnp.where(i < count, 1.0, 0.0).astype(jnp.float32)
+            live = jnp.where(i < count_ref[0, z], 1.0, 0.0).astype(jnp.float32)
             cur = cot[i, :, lo:lo + cols].astype(jnp.float32)
             rows = pl.ds(pl.multiple_of(i * per_image, per_image), per_image)
             delta[rows, :] = (cur * gelu_slope(pre) * live).astype(jnp.bfloat16)
@@ -235,17 +260,17 @@
         elif kind == "sum":
             total = part[k, j]
             if not first:
-                copy(k, j).wait_recv()
+                copy(k, j, me).wait_recv()
                 total = total + came[k, j].astype(jnp.float32)
             out[k, j] = total.astype(jnp.bfloat16)
-            copy(k, j).start()
+            copy(k, j, me + 1 if way == "u" else me - 1).start()
         elif kind == "fin":
             total = part[k, me]
             if me > 0:
-                u_copy(k, me).wait_recv()
+                u_copy(k, me, me).wait_recv()
                 total = total + u_in[k, me].astype(jnp.float32)
             if me < last:
-                d_copy(k, me).wait_recv()
+                d_copy(k, me, me).wait_recv()
                 total = total + d_in[k, me].astype(jnp.float32)
             stepped = par[:, k * cols:(k + 1) * cols] - learn_rate * total
             acc[k] = stepped
@@ -254,19 +279,8 @@
         elif kind == "merge":
             y_copy(k).wait_recv()
             stepped = acc[k]
-            merged[k] = stepped + mix * (far_in[k].astype(jnp.float32) - stepped)
-            out_copy(k).start()
-
-    _, orders = plan(n, [cols] * pieces, PRI, DEPTH)
-    segments = []
-    for order in orders:
-        parts = [[]]
-        for entry in order:
-            if entry[0] in ("norm", "comp"):
-                parts.append([])
-            else:
-                parts[-1].append(entry)
-        segments.append(parts)
+            out_ref[:, k * cols:(k + 1) * cols] = stepped + mix() * (far_in[k].astype(jnp.float32) - stepped)
+
     for stage in range(pieces + 2):
         for me in range(n):
             @pl.when(z == me)
@@ -278,26 +292,19 @@
         elif stage <= pieces:
             compute(stage - 1)
 
-    for k in range(pieces):
-        for s in range(n):
-            @pl.when((z < last) & (s <= z))
-            def _():
-                ag_copy(k, s, up, ag_up).wait_send()
-
-            @pl.when((z > 0) & (s >= z))
-            def _():
-                ag_copy(k, s, down, ag_dn).wait_send()
-
-            @pl.when(s > z)
-            def _():
-                u_copy(k, s).wait_send()
-
-            @pl.when(s < z)
-            def _():
-                d_copy(k, s).wait_send()
-
-        y_copy(k).wait_send()
-        out_copy(k).wait()
+    def drain(ref, send):
+        remote(ref, ref, send, y_recv.at[0], partner).wait_send()
+
+    for me in range(n):
+        @pl.when(z == me)
+        def _():
+            if me < last:
+                drain(wfull.at[:, :me + 1], ag_up)
+                drain(u_out.at[:, me + 1:], u_send)
+            if me > 0:
+                drain(wfull.at[:, me:], ag_dn)
+                drain(d_out.at[:, :me], d_send)
+    drain(far_out, y_send)
 
 
 def shards(n, reps, images, cotangent, params, counts, partner, ln_gain, ln_bias, expand_bias):
@@ -307,16 +314,15 @@
     cols = CHUNK
     pieces = hidden // cols
     rows = slots * per_image
-    scalars = pl.BlockSpec(memory_space=pltpu.SMEM)
     anywhere = pl.BlockSpec(memory_space=pl.ANY)
     dma = pltpu.SemaphoreType.DMA
     bf, f32 = jnp.bfloat16, jnp.float32
     piece = (pieces, n, depth, cols)
     merged = pl.pallas_call(
         functools.partial(body, n, reps, pieces),
-        out_shape=jax.ShapeDtypeStruct((depth, hidden), f32),
-        in_specs=[scalars] * 2 + [anywhere] * 6,
-        out_specs=anywhere,
+        out_shape=pltpu.VMEM((depth, hidden), f32),
+        in_specs=[pl.BlockSpec(memory_space=pltpu.SMEM)] + [anywhere] * 7,
+        out_specs=pl.BlockSpec(memory_space=pltpu.VMEM),
         scratch_shapes=[
             pltpu.VMEM((width,), f32),
             pltpu.VMEM((width,), f32),
@@ -336,14 +342,19 @@
             pltpu.VMEM((pieces, depth, cols), f32),
             pltpu.VMEM((pieces, depth, cols), bf),
             pltpu.VMEM((pieces, depth, cols), bf),
-            pltpu.VMEM((pieces, depth, cols), f32),
-            dma((6,)),
-        ] + [dma((pieces, n))] * 7 + [dma((pieces,))] * 3,
+            pltpu.SMEM((1, n), jnp.int32),
+            dma((8,)), dma((pieces, n + 1)), dma((pieces,)), dma((5,)),
+        ],
         compiler_params=pltpu.CompilerParams(
-            collective_id=0, has_side_effects=True, vmem_limit_bytes=62 * 1024 * 1024
+            collective_id=0, has_side_effects=True, vmem_limit_bytes=32 * 1024 * 1024
         ),
     )(
-        counts, partner, images[0], cotangent[0], params[0], ln_gain, ln_bias, expand_bias,
+        partner, *[
+            pltpu.with_memory_space_constraint(array, pltpu.HBM)
+            for array in (
+                counts, images[0], cotangent[0], params[0], ln_gain, ln_bias, expand_bias,
+            )
+        ],
     )
     return merged[None]
 

time: 70.3 us -> 65.1 us (0.926)
  Pallas kernels: 67.2 us -> 63.3 us
  local copies, waits for them, and re-layouts: 2.36 us -> 1.02 us
    pallas_call x1, Pallas kernels: 67.2 us -> 63.3 us  [shards(): pl.pallas_call(functools.partial(body, n, reps, pieces), out_shape=pltpu....]
    unnamed x1, local copies, waits for them, and re-layouts: 2.36 us -> 1.02 us
where the time goes in v1:
time: 65.1 us; the launch traced here: 64.9 us
  Pallas kernels  63.3 us (97%)
  local copies, waits for them, and re-layouts  1.02 us (2%)
  between operations  0.66 us (1%)
    pallas_call x1, Pallas kernels, shards(): pl.pallas_call(functools.partial(body, n, reps, pieces), out_shape=pltpu....  63.3 us

profile of v1, /device:TPU:0, one launch (start us, length us, event | category | flops | bytes accessed | tf_op | source)
XLA Modules:
  0.0 64.9 jit_solution(15097801356085394089)
XLA Ops:
  0.7 63.3 %shard_map.82 = f32[192,1536]{1,0:T(8,128)S(1)} custom-call(s32[1]{0:T(128)S(6)} %copy.11.partner_ref, s32[1,4]{1,0:T(1,128)} %count_in.1, bf16[4,128,768]{2,1,0:T(8,128)(2,1)} %bitcast.7, bf16[4,128,1536]{2,1,0:T(8,128)(2,1)} %bitcast.5, f32[192,1536]{1,0:T(8,128)} %bitcast.6, f32[768]{0:T(1024)} %gain_in.1, f32[768]{0:T(1024)} %bias_in.1, f32[1536]{0:T(1024)} %ebias_in.1), custom_call_target="tpu_custom_call" | custom-call | tf_op jit(solution)/shard_map/pallas_call | solution.py:321
  63.9 1.0 %copy.10 = f32[1,192,1536]{2,1,0:T(8,128)} copy(f32[1,192,1536]{2,1,0:T(8,128)S(1)} %bitcast.4) | data formatting | bytes 2359296

commit v2 on v1

--- a/solution.py
+++ b/solution.py
@@ -11,14 +11,14 @@
 learn_rate = 0.5
 CHUNK = 128
 DEPTH = 1.0
+MIXED = (1, 5, 8)
 PRI = dict(
-    own=-13.95, fwd=-13.04, fwd_far=-4.93, comp=-1.0, sum=-2.09, sum_far=-6.79, sum_hop=13.66,
-    fin=-5.34, merge=-2.93, norm=10.81,
+    give=192.27, take=-47.75, late=95.14, own=-10.17, fwd=-5.93, fwd_far=-0.75, comp=50.94, sum=78.09, sum_far=-82.25, sum_hop=50.75, fin=-114.91, merge=-80.50, norm=68.37,
 )
 MESH_ID = pl.DeviceIdType.MESH
 
 
-def plan(n, widths, pri, depth, rate=120.0, lat=2.2, cost=0.06):
+def plan(n, widths, pri, depth, mixed, rate=125.0, lat=2.5, cost=0.055):
     last = n - 1
     pieces = len(widths)
     dur = [w / rate + cost for w in widths]
@@ -37,7 +37,11 @@
             for j in range(z + 1, n): mine.append(("sum", k, j, "u"))
             for j in range(z): mine.append(("sum", k, j, "d"))
             mine.append(("fin", k, z, "y"))
-            mine.append(("merge", k, z, ""))
+            if k in mixed:
+                mine.append(("give", k, z, "y"))
+                mine.append(("take", k, z, ""))
+            else:
+                mine.append(("merge", k, z, ""))
         mine.append(("norm", 0, 0, ""))
         todo.append(mine)
     done = [set() for _ in range(n)]
@@ -46,7 +50,7 @@
         far = abs(j - z)
         if kind == "own": return k + pri["own"]
         if kind == "fwd": return k + pri["fwd"] + (far - 1) * pri["fwd_far"]
-        if kind == "sum": return k + pri["sum"] + far * pri["sum_far"] + (z if way == "u" else last - z) * pri["sum_hop"]
+        if kind == "sum": return k + (pri["late"] if k in mixed else 0.0) + pri["sum"] + far * pri["sum_far"] + (z if way == "u" else last - z) * pri["sum_hop"]
         return k + pri.get(kind, 0.0)
     def ready(z, t):
         kind, k, j, way = t
@@ -60,14 +64,15 @@
             if k and ("comp", k - 1, 0, "") not in d: return inf
             for s in range(n):
                 if s != z and ("fwd", k, s, "u" if s < z else "d") not in d: return inf
-        elif kind in ("sum", "fin"):
+        elif kind in ("sum", "fin", "give"):
             if ("comp", k, 0, "") not in d: return inf
+            if k in mixed and kind != "give" and ("take", k, z, "") not in d: return inf
             if kind == "sum" and (z > 0 if way == "u" else z < last): times.append(a.get((way, k, j), inf))
             if kind == "fin":
                 if z > 0: times.append(a.get(("u", k, z), inf))
                 if z < last: times.append(a.get(("d", k, z), inf))
-        elif kind == "merge":
-            if ("fin", k, z, "y") not in d: return inf
+        elif kind in ("merge", "take"):
+            if ("fin" if kind == "merge" else "give", k, z, "y") not in d: return inf
             times.append(a.get(("y", k, z), inf))
         sends = kind in ("own", "sum") or (kind == "fwd" and (z < last if way == "u" else z > 0))
         if sends: times.append(link[z][way] - depth * dur[k])
@@ -84,16 +89,17 @@
         t0, z, t = best
         kind, k, j, way = t
         todo[z].remove(t); done[z].add(t); orders[z].append(t)
-        spend = {"own": .03, "fwd": .05, "comp": widths[k] / 110.0, "sum": .12, "fin": .15, "merge": .15, "norm": 2.0}[kind]
+        spend = {"own": .03, "fwd": .05, "comp": widths[k] / 75.0, "sum": .05, "fin": .05, "merge": .05, "norm": 0.9, "give": .15, "take": .2}[kind]
         now[z] = t0 + spend
         to = None
         if kind == "own" or kind == "fwd": to, tag = z + (1 if way == "u" else -1), ("a", k, j)
         elif kind == "sum": to, tag = z + (1 if way == "u" else -1), (way, k, j)
-        elif kind == "fin": to, tag = z, ("y", k, z)
+        elif kind == "give" or (kind == "fin" and k not in mixed): to, tag = z, ("y", k, z)
         if to is not None and 0 <= to <= last:
             start = max(link[z][way], now[z])
-            link[z][way] = start + dur[k]
-            arrive[to][tag] = start + dur[k] + lat
+            took = dur[k] * (n + 1 if kind == "give" else 1)
+            link[z][way] = start + took
+            arrive[to][tag] = start + took + lat
     return max(now), orders
 
 
@@ -103,11 +109,11 @@
 
 
 def body(
-    n, reps, pieces,
+    n, reps, pieces, mixed,
     partner_ref, count_in, images, cotangent, weights, gain_in, bias_in, ebias_in,
     out_ref,
     gain_ref, bias_ref, ebias_ref, img, cot, par, x, xt, wfull, delta, part, u_in, d_in, u_out, d_out, acc,
-    far_out, far_in,
+    far_out, far_in, mix_out, mix_in,
     count_ref, in_sem, z_recv, y_recv, sent,
 ):
     z = lax.axis_index("fsdp")
@@ -120,7 +126,7 @@
     cols = wfull.shape[-1]
     scale = float(width) ** (-0.5)
 
-    _, orders = plan(n, [cols] * pieces, PRI, DEPTH)
+    _, orders = plan(n, [cols] * pieces, PRI, DEPTH, mixed)
     segments = []
     for order in orders:
         parts = [[]]
@@ -196,6 +202,10 @@
 
     def y_copy(k):
         return remote(far_out.at[k], far_in.at[k], y_send, y_recv.at[k], partner)
+
+    def x_copy(k):
+        i = mixed.index(k)
+        return remote(mix_out.at[i], mix_in.at[i], y_send, y_recv.at[k], partner)
 
     def norm():
         load_rest.wait()
@@ -224,27 +234,18 @@
         w = wfull.at[k]
         extra = ebias_ref[lo:lo + cols][None, :]
 
-        def one(i, carry):
-            pre = jnp.dot(
-                x[i], w[...].reshape(width, cols), preferred_element_type=jnp.float32
-            )
+        count = count_ref[0, z]
+        table = w[...].reshape(width, cols)
+        for i in range(slots):
+            pre = jnp.dot(x[i], table, preferred_element_type=jnp.float32)
             pre = pre * scale + extra
-            live = jnp.where(i < count_ref[0, z], 1.0, 0.0).astype(jnp.float32)
+            live = jnp.where(i < count, 1.0, 0.0).astype(jnp.float32)
             cur = cot[i, :, lo:lo + cols].astype(jnp.float32)
-            rows = pl.ds(pl.multiple_of(i * per_image, per_image), per_image)
-            delta[rows, :] = (cur * gelu_slope(pre) * live).astype(jnp.bfloat16)
-            return carry
-
-        lax.fori_loop(0, slots, one, 0)
-
-        def two(j, carry):
-            rows = pl.ds(pl.multiple_of(j * depth, depth), depth)
-            part[k, j] = scale * jnp.dot(
-                xt[rows, :], delta[...], preferred_element_type=jnp.float32
-            )
-            return carry
-
-        lax.fori_loop(0, n, two, 0)
+            delta[i * per_image:(i + 1) * per_image, :] = (
+                cur * gelu_slope(pre) * live
+            ).astype(jnp.bfloat16)
+        terms = scale * jnp.dot(xt[...], delta[...], preferred_element_type=jnp.float32)
+        part[k] = terms.reshape(n, depth, cols)
 
     def step(me, kind, k, j, way):
         to, send = (up, ag_up) if way == "u" else (down, ag_dn)
@@ -272,10 +273,25 @@
             if me < last:
                 d_copy(k, me, me).wait_recv()
                 total = total + d_in[k, me].astype(jnp.float32)
-            stepped = par[:, k * cols:(k + 1) * cols] - learn_rate * total
+            own = par[:, k * cols:(k + 1) * cols]
+            if k in mixed:
+                own = own + mix() * (mix_in[mixed.index(k), n].astype(jnp.float32) - own)
+                out_ref[:, k * cols:(k + 1) * cols] = own - learn_rate * total
+                return
+            stepped = own - learn_rate * total
             acc[k] = stepped
             far_out[k] = stepped.astype(jnp.bfloat16)
             y_copy(k).start()
+        elif kind == "give":
+            for i in range(n):
+                mix_out[mixed.index(k), i] = part[k, i].astype(jnp.bfloat16)
+            mix_out[mixed.index(k), n] = wfull[k, me]
+            x_copy(k).start()
+        elif kind == "take":
+            x_copy(k).wait_recv()
+            for i in range(n):
+                mine = part[k, i]
+                part[k, i] = mine + mix() * (mix_in[mixed.index(k), i].astype(jnp.float32) - mine)
         elif kind == "merge":
             y_copy(k).wait_recv()
             stepped = acc[k]
@@ -304,7 +320,9 @@
             if me > 0:
                 drain(wfull.at[:, me:], ag_dn)
                 drain(d_out.at[:, :me], d_send)
-    drain(far_out, y_send)
+    drain(far_out.at[len(mixed):], y_send)
+    if mixed:
+        drain(mix_out, y_send)
 
 
 def shards(n, reps, images, cotangent, params, counts, partner, ln_gain, ln_bias, expand_bias):
@@ -313,13 +331,14 @@
     depth = params.shape[1]
     cols = CHUNK
     pieces = hidden // cols
+    mixed = tuple(k for k in MIXED if k < pieces)
     rows = slots * per_image
     anywhere = pl.BlockSpec(memory_space=pl.ANY)
     dma = pltpu.SemaphoreType.DMA
     bf, f32 = jnp.bfloat16, jnp.float32
     piece = (pieces, n, depth, cols)
     merged = pl.pallas_call(
-        functools.partial(body, n, reps, pieces),
+        functools.partial(body, n, reps, pieces, mixed),
         out_shape=pltpu.VMEM((depth, hidden), f32),
         in_specs=[pl.BlockSpec(memory_space=pltpu.SMEM)] + [anywhere] * 7,
         out_specs=pl.BlockSpec(memory_space=pltpu.VMEM),
@@ -342,6 +361,8 @@
             pltpu.VMEM((pieces, depth, cols), f32),
             pltpu.VMEM((pieces, depth, cols), bf),
             pltpu.VMEM((pieces, depth, cols), bf),
+            pltpu.VMEM((len(mixed), n + 1, depth, cols), bf),
+            pltpu.VMEM((len(mixed), n + 1, depth, cols), bf),
             pltpu.SMEM((1, n), jnp.int32),
             dma((8,)), dma((pieces, n + 1)), dma((pieces,)), dma((5,)),
         ],

time: 65.1 us -> 62.4 us (0.959)
  Pallas kernels: 63.3 us -> 60.5 us
    pallas_call x1, Pallas kernels: 63.3 us -> 60.5 us  [shards(): pl.pallas_call(functools.partial(body, n, reps, pieces, mixed), out_shape...]
where the time goes in v2:
time: 62.4 us; the launch traced here: 62.2 us
  Pallas kernels  60.5 us (97%)
  local copies, waits for them, and re-layouts  1.02 us (2%)
  between operations  0.66 us (1%)
    pallas_call x1, Pallas kernels, shards(): pl.pallas_call(functools.partial(body, n, reps, pieces, mixed), out_shape...  60.5 us

profile of v2, /device:TPU:0, one launch (start us, length us, event | category | flops | bytes accessed | tf_op | source)
XLA Modules:
  0.0 62.2 jit_solution(12419521540441762147)
XLA Ops:
  0.7 60.5 %shard_map.82 = f32[192,1536]{1,0:T(8,128)S(1)} custom-call(s32[1]{0:T(128)S(6)} %copy.11.partner_ref, s32[1,4]{1,0:T(1,128)} %count_in.1, bf16[4,128,768]{2,1,0:T(8,128)(2,1)} %bitcast.7, bf16[4,128,1536]{2,1,0:T(8,128)(2,1)} %bitcast.5, f32[192,1536]{1,0:T(8,128)} %bitcast.6, f32[768]{0:T(1024)} %gain_in.1, f32[768]{0:T(1024)} %bias_in.1, f32[1536]{0:T(1024)} %ebias_in.1), custom_call_target="tpu_custom_call" | custom-call | tf_op jit(solution)/shard_map/pallas_call | solution.py:340
  61.2 1.0 %copy.10 = f32[1,192,1536]{2,1,0:T(8,128)} copy(f32[1,192,1536]{2,1,0:T(8,128)S(1)} %bitcast.4) | data formatting | bytes 2359296

commit v3 on v2

--- a/solution.py
+++ b/solution.py
@@ -10,15 +10,16 @@
 eps_norm = 1e-06
 learn_rate = 0.5
 CHUNK = 128
-DEPTH = 1.0
-MIXED = (1, 5, 8)
+DEPTH = 0.00
+MIXED = (2, 4, 9,)
 PRI = dict(
-    give=192.27, take=-47.75, late=95.14, own=-10.17, fwd=-5.93, fwd_far=-0.75, comp=50.94, sum=78.09, sum_far=-82.25, sum_hop=50.75, fin=-114.91, merge=-80.50, norm=68.37,
+    give=21.89, take=-114.92, late=96.59, own=24.29, fwd=23.89, fwd_far=-122.00, comp=9.92,
+    sum=200.38, sum_far=-215.30, sum_hop=270.01, fin=-88.99, merge=67.96, norm=403.70,
 )
 MESH_ID = pl.DeviceIdType.MESH
 
 
-def plan(n, widths, pri, depth, mixed, rate=125.0, lat=2.5, cost=0.055):
+def plan(n, widths, pri, depth, mixed, rate=126.2, lat=2.43, cost=0.055):
     last = n - 1
     pieces = len(widths)
     dur = [w / rate + cost for w in widths]
@@ -89,7 +90,7 @@
         t0, z, t = best
         kind, k, j, way = t
         todo[z].remove(t); done[z].add(t); orders[z].append(t)
-        spend = {"own": .03, "fwd": .05, "comp": widths[k] / 75.0, "sum": .05, "fin": .05, "merge": .05, "norm": 0.9, "give": .15, "take": .2}[kind]
+        spend = {"own": .03, "fwd": .05, "comp": widths[k] / 142.0, "sum": .05, "fin": .05, "merge": .05, "norm": 0.9, "give": .07, "take": .1}[kind]
         now[z] = t0 + spend
         to = None
         if kind == "own" or kind == "fwd": to, tag = z + (1 if way == "u" else -1), ("a", k, j)

time: 62.4 us -> 62.4 us (level)
  no operation moved by 1% of the time
where the time goes in v3:
time: 62.4 us; the launch traced here: 62.3 us
  Pallas kernels  60.6 us (97%)
  local copies, waits for them, and re-layouts  1.02 us (2%)
  between operations  0.66 us (1%)
    pallas_call x1, Pallas kernels, shards(): pl.pallas_call(functools.partial(body, n, reps, pieces, mixed), out_shape...  60.6 us

profile of v3, /device:TPU:0, one launch (start us, length us, event | category | flops | bytes accessed | tf_op | source)
XLA Modules:
  0.0 62.3 jit_solution(8682906518989846500)
XLA Ops:
  0.7 60.6 %shard_map.82 = f32[192,1536]{1,0:T(8,128)S(1)} custom-call(s32[1]{0:T(128)S(6)} %copy.11.partner_ref, s32[1,4]{1,0:T(1,128)} %count_in.1, bf16[4,128,768]{2,1,0:T(8,128)(2,1)} %bitcast.7, bf16[4,128,1536]{2,1,0:T(8,128)(2,1)} %bitcast.5, f32[192,1536]{1,0:T(8,128)} %bitcast.6, f32[768]{0:T(1024)} %gain_in.1, f32[768]{0:T(1024)} %bias_in.1, f32[1536]{0:T(1024)} %ebias_in.1), custom_call_target="tpu_custom_call" | custom-call | tf_op jit(solution)/shard_map/pallas_call | solution.py:341
  61.3 1.0 %copy.10 = f32[1,192,1536]{2,1,0:T(8,128)} copy(f32[1,192,1536]{2,1,0:T(8,128)S(1)} %bitcast.4) | data formatting | bytes 2359296
